TPU v7x, 32 devices: a whole 2x2x4 slice. The times are simulated.
32 devices in a mesh: lat: 8 (over z, y), lev: 4 (over x, core).
Axes of the slice: x: 2, y: 2, z: 4, core: 2. Of those that a mesh axis runs over, the one named last changes fastest.
Arguments:
- field: float32 [4, 320, 4096], P(None, 'lat', 'lev'), may hold values from -6 to 6
- weights: bfloat16 [4, 320, 4096], P(None, 'lat', 'lev'), may hold values from 0 to 0.5
- depart_row: int32 [320, 4096], P('lat', 'lev'), may hold values from -2 to 1
- depart_col: int32 [320, 4096], P('lat', 'lev'), may hold values from -2 to 1
- legendre: bfloat16 [320, 16, 640], P('lat'), may hold values from -6 to 6
- wave_slot: int32 [16], replicated, may hold values from 0 to 15, each once
Outputs:
- updated: float32 [4, 320, 4096], P(None, 'lat', 'lev')
- spectral: float32 [16, 2, 4, 2, 640], P('lat', None, 'lev')
Inputs may be any that keep to these rules, and one draw needn't show every extreme that they name: `depart_row`: latitude offsets of departure cells, so that rows i - 2 to i + 2 are read. `depart_col`: longitude offsets of departure cells, so that columns j - 2 to j + 2 are read, periodically. `wave_slot`: A permutation of 0 to 15.
All inputs are finite; a program needn't handle non-finite values.
Results may differ from a plain program's by a relative error of at most 0.0033.
Values may be sent and summed in bfloat16 or wider, within the bound.
A program may use at most 128 MiB of HBM per device.

v0:
```python
import math
import jax
import jax.numpy as jnp
from jax import lax
from jax.sharding import PartitionSpec as P

NLON = 4096
NT = 1279
M_OWN = 2
DAMPING = 4.0


def padded(array, sides, width, wrap):
    for axis, dim in sides:
        size, length = (lax.axis_size(axis), array.shape[dim])
        up = [(i, (i + 1) % size) for i in range(size if wrap else size - 1)]
        down = [(j, i) for i, j in up]
        last = lax.slice_in_dim(array, length - width, length, axis=dim)
        initial = lax.slice_in_dim(array, 0, width, axis=dim)
        before = lax.ppermute(last, axis, up)
        after = lax.ppermute(initial, axis, down)
        array = jnp.concatenate([before, array, after], axis=dim)
    return array


def swapped(value, axis, apart):
    mask = 2**apart
    pairs = [(source, source ^ mask) for source in range(lax.axis_size(axis))]
    return lax.ppermute(value, axis, pairs)


def forward_table(lon_list, wave_list):
    phases = lon_list[:, None] * wave_list[None, :] % NLON
    angles = phases.astype(jnp.float32) * (2.0 * math.pi / NLON)
    return jnp.concatenate([jnp.cos(angles), -jnp.sin(angles)], axis=1) * (1.0 / math.sqrt(NLON))


def inverse_table(wave_list, lon_list, wave_count):
    phases = wave_list[:, None] * lon_list[None, :] % NLON
    angles = phases.astype(jnp.float32) * (2.0 * math.pi / NLON)
    weight = (jnp.where(wave_list == 0, 1.0, 2.0) / math.sqrt(wave_count))[:, None]
    return jnp.concatenate([weight * jnp.cos(angles), -weight * jnp.sin(angles)], axis=0)


def diffuse(raw_sums, slot_waves, steps_count):
    degree = (
        slot_waves[:, None, None]
        + 2 * jnp.arange(steps_count, dtype=jnp.int32)[None, None, :]
        + jnp.arange(2, dtype=jnp.int32)[None, :, None]
    )
    inside = degree <= NT
    factor = 1.0 / (
        1.0 + DAMPING * (degree * (degree + 1)).astype(jnp.float32) / float(NT * (NT + 1))
    )
    masked = jnp.where(inside[:, :, None, None, :], raw_sums, jnp.zeros_like(raw_sums))
    damped = masked * factor[:, :, None, None, :]
    return (damped, (damped - masked).astype(jnp.bfloat16))


def on_device(field, weights, depart_row, depart_col, legendre, wave_slot):
    hp = lax.Precision.HIGHEST
    lat_count = lax.axis_size("lat")
    lev_count = lax.axis_size("lev")
    lat_here = lax.axis_index("lat")
    levels, rows_here, lon_width = field.shape
    lev_local = levels // lev_count
    wave_count = M_OWN * lat_count
    steps_count = legendre.shape[2]
    half_lat = rows_here * lat_count // 2
    northern = lat_here < lat_count // 2
    bit_count = lat_count.bit_length() - 1
    band = padded(field, (("lat", 1),), 2, False)
    padded_block = padded(band, (("lev", 2),), 2, True)
    wide_cols = lon_width + 4
    flattened = padded_block.reshape(levels, (rows_here + 4) * wide_cols)
    row_base = jnp.arange(rows_here, dtype=jnp.int32)[:, None] + 2 + depart_row
    col_base = jnp.arange(lon_width, dtype=jnp.int32)[None, :] + 2 + depart_col
    summed = jnp.zeros((levels, rows_here * lon_width), jnp.float32)
    for row_step in range(2):
        for col_step in range(2):
            source = ((row_base + row_step) * wide_cols + col_base + col_step).reshape(-1)
            corner = weights[2 * row_step + col_step].reshape(-1).astype(jnp.float32)
            summed = summed + corner[None, :] * jnp.take(flattened, source, axis=1)
    advected = summed.reshape(levels, rows_here, lon_width)
    wavenumbers = jnp.arange(wave_count, dtype=jnp.int32) * (NT + 1) // wave_count
    one_hot = (wave_slot[None, :] == jnp.arange(wave_count, dtype=jnp.int32)[:, None]).astype(
        jnp.int32
    )
    k_of_slot = jnp.sum(one_hot * jnp.arange(wave_count, dtype=jnp.int32)[None, :], axis=1)
    slot_waves = jnp.sum(one_hot * wavenumbers[None, :], axis=1)
    columns = lax.all_to_all(advected, "lev", split_axis=0, concat_axis=2, tiled=True)
    wave_table = forward_table(jnp.arange(NLON, dtype=jnp.int32), wavenumbers)
    coeffs = jnp.dot(
        columns.reshape(-1, NLON), wave_table, precision=hp, preferred_element_type=jnp.float32
    )
    fourier = coeffs.reshape(lev_local, rows_here, 2, wave_count).astype(jnp.bfloat16)
    partner = fourier
    for bit_number in range(bit_count):
        partner = swapped(partner, "lat", bit_number)
    partner = jnp.flip(partner, axis=1)
    forward_scale = 1.0 / math.sqrt(half_lat)
    parity = jnp.where(northern, 0, 1).astype(jnp.int32)
    inverse_scale = 1.0 / math.sqrt(steps_count)
    chosen = k_of_slot
    leg_part = jnp.take(legendre, chosen, axis=1)
    own_part = jnp.take(fourier, chosen, axis=3)
    other_part = jnp.take(partner, chosen, axis=3)
    own_term = jnp.einsum("lkj,vlck->kvcj", leg_part, own_part, preferred_element_type=jnp.float32)
    other_term = jnp.einsum(
        "lkj,vlck->kvcj", leg_part, other_part, preferred_element_type=jnp.float32
    )
    combined = jnp.where(northern, own_term + other_term, other_term - own_term) * forward_scale
    nothing = jnp.zeros_like(combined)
    owned_sums = lax.psum_scatter(
        jnp.stack(
            [jnp.where(northern, combined, nothing), jnp.where(northern, nothing, combined)], axis=1
        ),
        "lat",
        scatter_dimension=0,
        tiled=True,
    )
    own_waves = lax.dynamic_slice_in_dim(slot_waves, lat_here * M_OWN, M_OWN, 0)
    damped, change = diffuse(owned_sums, own_waves, steps_count)
    chosen = k_of_slot
    leg_part = jnp.take(legendre, chosen, axis=1)
    own_parity = lax.dynamic_index_in_dim(
        lax.all_gather(change, "lat", axis=0, tiled=True), parity, 1, keepdims=False
    )
    result = jnp.einsum("lkj,kvcj->vlck", leg_part, own_parity, preferred_element_type=jnp.float32)
    half_sum = result * inverse_scale
    across = half_sum
    for bit_number in range(bit_count):
        across = swapped(across, "lat", bit_number)
    across = jnp.flip(across, axis=1)
    synthesis = jnp.where(northern, half_sum + across, across - half_sum)
    synthesis = synthesis.reshape(lev_local, rows_here, 2 * wave_count)
    back_table = inverse_table(slot_waves, jnp.arange(NLON, dtype=jnp.int32), wave_count)
    circles = jnp.dot(
        synthesis.reshape(-1, 2 * wave_count),
        back_table,
        precision=hp,
        preferred_element_type=jnp.float32,
    ).reshape(lev_local, rows_here, NLON)
    increment = lax.all_to_all(circles, "lev", split_axis=2, concat_axis=0, tiled=True)
    updated = advected + increment
    return (updated, damped)


def solution(mesh):
    placed = (
        P(None, "lat", "lev"),
        P(None, "lat", "lev"),
        P("lat", "lev"),
        P("lat", "lev"),
        P("lat", None, None),
        P(),
    )
    return jax.shard_map(
        on_device,
        mesh=mesh,
        in_specs=placed,
        out_specs=(P(None, "lat", "lev"), P("lat", None, "lev", None, None)),
        check_vma=False,
    )
```

profile of v0, /device:TPU:0, one launch (start us, length us, event | category | flops | bytes accessed | tf_op | source)
XLA Modules:
  0.0 875.8 jit_solution(8156510227616605305)
XLA Ops:
  7.2 1.1 fusion.52
  8.3 4.9 collective-permute-start
  13.2 1.3 collective-permute-start.1
  14.5 1.1 fusion.43
  15.6 0.7 fusion.27
  16.6 0.7 fusion.25
  17.3 0.7 fusion.26
  18.0 0.7 compare_and_fusion.2
  18.8 1.1 convert_bitcast_fusion.3
  19.8 1.9 fusion.29
  21.8 1.3 select_reduce_fusion.1
  23.6 1.2 pad_maximum_fusion
  24.8 0.7 fusion.51
  25.5 1.7 collective-permute-start.3
  28.0 0.7 copy.106
  28.7 0.7 copy.108
  29.4 0.7 copy.110
  30.1 3.0 gather_fusion.5
  33.7 1.4 concatenate.13
  35.1 0.8 reshape.196
  35.9 11.3 %copy.81 = f32[4,45232]{0,1:T(8,128)} copy(f32[4,45232]{1,0:T(4,128)S(1)} %reshape.196) | data formatting | bytes 1447424 | tf_op jit(solution)/shard_map/reshape | solution.py:75
  47.2 142.5 %gather_fusion = f32[40960,4]{1,0:T(8,128)} fusion(f32[4,45232]{0,1:T(8,128)} %copy.81, s32[40960]{0:T(1024)S(1)} %copy-done.4), kind=kCustom, calls=%fused_computation.clone | custom fusion | bytes 1474560 | tf_op jit(solution)/shard_map/jit(_take)/gather | solution.py:83
  189.7 11.4 %copy.82 = f32[40960,4]{0,1:T(4,128)S(1)} copy(f32[40960,4]{1,0:T(8,128)} %gather_fusion) | data formatting | bytes 1310720 | tf_op jit(solution)/shard_map/jit(_take)/gather | solution.py:83
  201.1 142.5 %gather_fusion.1 = f32[40960,4]{1,0:T(8,128)} fusion(f32[4,45232]{0,1:T(8,128)} %copy.81, s32[40960]{0:T(1024)S(1)} %copy-done.5), kind=kCustom, calls=%fused_computation.3.clone | custom fusion | bytes 1474560 | tf_op jit(solution)/shard_map/jit(_take)/gather | solution.py:83
  343.6 11.4 %copy.84 = f32[40960,4]{0,1:T(4,128)S(1)} copy(f32[40960,4]{1,0:T(8,128)} %gather_fusion.1) | data formatting | bytes 1310720 | tf_op jit(solution)/shard_map/jit(_take)/gather | solution.py:83
  355.1 142.5 %gather_fusion.2 = f32[40960,4]{1,0:T(8,128)} fusion(f32[4,45232]{0,1:T(8,128)} %copy.81, s32[40960]{0:T(1024)S(1)} %copy-done.3), kind=kCustom, calls=%fused_computation.4.clone | custom fusion | bytes 1474560 | tf_op jit(solution)/shard_map/jit(_take)/gather | solution.py:83
  497.6 12.2 %copy.86 = f32[40960,4]{0,1:T(4,128)} copy(f32[40960,4]{1,0:T(8,128)} %gather_fusion.2) | data formatting | bytes 1310720 | tf_op jit(solution)/shard_map/jit(_take)/gather | solution.py:83
  509.7 142.5 %gather_fusion.3 = f32[40960,4]{1,0:T(8,128)} fusion(f32[4,45232]{0,1:T(8,128)} %copy.81, s32[40960]{0:T(1024)S(1)} %fusion.28), kind=kCustom, calls=%fused_computation.5.clone | custom fusion | bytes 1474560 | tf_op jit(solution)/shard_map/jit(_take)/gather | solution.py:83
  652.3 12.2 %copy.88 = f32[40960,4]{0,1:T(4,128)} copy(f32[40960,4]{1,0:T(8,128)} %gather_fusion.3) | data formatting | bytes 1310720 | tf_op jit(solution)/shard_map/jit(_take)/gather | solution.py:83
  664.5 2.4 fusion.1
  666.9 0.8 copy-done.2
  667.7 1.2 copy.124
  668.9 3.5 all-to-all-start
  672.8 1.1 maximum_multiply_fusion
  673.9 8.7 all-to-all-done
  684.1 2.7 collective-permute-start.4
  686.8 0.7 dynamic_slice.7
  687.5 0.9 collective-permute-done.4
  688.5 3.0 collective-permute-start.5
  691.5 1.6 collective-permute-done.5
  693.1 3.0 collective-permute-start.6
  696.1 1.3 dynamic-slice
  698.2 0.7 gather_fusion.4
  699.0 0.7 gather_fusion.6
  699.7 0.9 fusion.5
  700.7 0.9 select_bitcast_fusion.2
  701.6 0.7 pad_maximum_fusion.1
  702.4 68.8 %all-reduce.3.cloned.1.call-done = f32[16,2,1,2,640]{4,3,0,2,1:T(2,128)} async-done(((f32[16,2,1,2,640]{4,3,0,2,1:T(2,128)}), f32[16,2,1,2,640]{4,3,0,2,1:T(2,128)}) %all-reduce.3.cloned.1.call-update) | async-done | bytes 163856
  771.2 0.8 subtract_convert_fusion
  771.9 30.6 %all_gather.3 = bf16[16,2,1,2,640]{4,3,0,2,1:T(2,128)(2,1)S(1)} all-gather(bf16[2,2,1,2,640]{4,3,0,2,1:T(2,128)(2,1)S(1)} %get-tuple-element.19), channel_id=1, replica_groups=mesh['lat'=8,'lev'=4] {'lat'}, dimensions={0}, use_global_device_ids=true | all-gather | bytes 92160 | tf_op jit(solution)/shard_map/all_gather | solution.py:127
  803.3 3.3 collective-permute-done.7
  807.3 3.1 collective-permute-done.8
  810.6 1.7 cosine_multiply_fusion
  812.3 2.7 collective-permute-done.9
  815.2 3.4 fusion.9
  819.2 19.4 %reduce = f32[4096,40]{1,0:T(8,128)} reduce(f32[4096,1,40]{2,1,0:T(1,128)S(1)} %bitcast.113, f32[]{:T(128)} %broadcast.351), dimensions={1}, to_apply=%bitcast.100.reduce_sub_computation | reduce | bytes 1310724
  838.6 3.9 reshape.301
  842.5 3.7 all-to-all-start.1
  846.9 9.4 %all-to-all-done.1 = f32[4,1,40960]{2,1,0:T(1,128)S(1)} async-done(((f32[4,1,40960]{2,1,0:T(1,128)}), f32[4,1,40960]{2,1,0:T(1,128)S(1)}, u32[]{:S(2)}, u32[]{:S(2)}) %all-to-all-start.1) | async-done | bytes 655392 | tf_op jit(solution)/shard_map/all_to_all | solution.py:144
  856.2 3.4 reduce.1
  859.6 5.1 reshape.302
  864.7 1.6 copy.101
  866.3 1.5 bitcast_add_fusion
  867.7 1.2 copy.99
  (63 shorter events, 7.3 us)
Async XLA Ops:
  7.2 22.9 %copy-start = (bf16[40,16,640]{2,1,0:T(8,128)(2,1)S(1)}, bf16[40,16,640]{2,1,0:T(8,128)(2,1)}, u32[]{:S(2)}) copy-start(bf16[40,16,640]{2,1,0:T(8,128)(2,1)} %param.16) | copy-start | bytes 2457604
  8.3 15.3 %collective-permute-start = (f32[4,2,1024]{2,1,0:T(2,128)S(1)}, f32[4,2,1024]{2,1,0:T(2,128)S(1)}, u32[]{:S(2)}, u32[]{:S(2)}) collective-permute-start(f32[4,2,1024]{2,1,0:T(2,128)S(1)} %get-tuple-element.23), channel_id=1, source_target_pairs={{0,4},{4,8},{8,12},{12,16},{16,20},{20,24},{24,28},{1,5},{5,9},{9,... | collective-permute-start | bytes 98312 | tf_op jit(solution)/shard_map/ppermute | solution.py:20
  13.2 10.4 %collective-permute-start.1 = (f32[4,2,1024]{2,1,0:T(2,128)S(1)}, f32[4,2,1024]{2,1,0:T(2,128)S(1)}, u32[]{:S(2)}, u32[]{:S(2)}) collective-permute-start(f32[4,2,1024]{2,1,0:T(2,128)S(1)} %get-tuple-element.24), channel_id=1, source_target_pairs={{4,0},{8,4},{12,8},{16,12},{20,16},{24,20},{28,24},{5,1},{9,5},{13... | collective-permute-start | bytes 98312 | tf_op jit(solution)/shard_map/ppermute | solution.py:21
  25.5 7.5 collective-permute-start.2
  25.5 8.2 collective-permute-start.3
  27.3 5.8 copy-start.9
  33.0 14.1 %copy-start.4 = (s32[40960]{0:T(1024)S(1)}, s32[40960]{0:T(1024)}, u32[]{:S(2)}) copy-start(s32[40960]{0:T(1024)} %fusion.25) | copy-start | bytes 491524
  33.1 0.7 copy-start.8
  35.9 165.2 %copy-start.5 = (s32[40960]{0:T(1024)S(1)}, s32[40960]{0:T(1024)}, u32[]{:S(2)}) copy-start(s32[40960]{0:T(1024)} %fusion.26) | copy-start | bytes 491524
  189.7 165.4 %copy-start.3 = (s32[40960]{0:T(1024)S(1)}, s32[40960]{0:T(1024)}, u32[]{:S(2)}) copy-start(s32[40960]{0:T(1024)} %fusion.27) | copy-start | bytes 491524
  497.6 166.9 %copy-start.6 = (f32[5,8,8,128]{3,1,2,0:T(8,128)S(1)}, f32[5,8,8,128]{3,1,2,0:T(8,128)}, u32[]{:S(2)}) copy-start(f32[5,8,8,128]{3,1,2,0:T(8,128)} %copy.104) | copy-start | bytes 491524
  497.6 166.9 %copy-start.7 = (f32[5,8,8,128]{3,1,2,0:T(8,128)S(1)}, f32[5,8,8,128]{3,1,2,0:T(8,128)}, u32[]{:S(2)}) copy-start(f32[5,8,8,128]{3,1,2,0:T(8,128)} %copy.106) | copy-start | bytes 491524
  509.7 162.9 %copy-start.10 = (pred[16]{0:T(512)(128)(4,1)S(1)}, pred[16]{0:T(512)(128)(4,1)}, u32[]{:S(2)}) copy-start(pred[16]{0:T(512)(128)(4,1)} %compare_and_fusion.4) | copy-start | bytes 52
  652.2 216.7 %copy-start.1 = (bf16[40,16,640]{2,1,0:T(8,128)(2,1)S(1)}, bf16[40,16,640]{2,1,0:T(8,128)(2,1)}, u32[]{:S(2)}) copy-start(bf16[40,16,640]{2,1,0:T(8,128)(2,1)} %param.16) | copy-start | bytes 2457604
  666.8 0.8 copy-start.2
  668.9 13.7 %all-to-all-start = ((f32[4,40,1024]{2,1,0:T(8,128)}), f32[4,40,1024]{2,1,0:T(8,128)S(1)}, u32[]{:S(2)}, u32[]{:S(2)}) async-start(f32[4,40,1024]{2,1,0:T(8,128)} %bitcast.109), calls=%async_computation | async-start | bytes 1310720 | tf_op jit(solution)/shard_map/all_to_all | solution.py:91
  672.4 98.8 %all-reduce.3.cloned.1.call-start = ((), (), s32[]{:S(2)}) async-start(), calls=%async_computation.2 | async-start | bytes 327680
  684.1 4.3 collective-permute-start.4
  688.5 4.6 collective-permute-start.5
  693.1 5.8 collective-permute-start.6
  802.9 3.8 collective-permute-start.7
  806.6 3.7 collective-permute-start.8
  810.4 4.6 collective-permute-start.9
  842.5 13.7 %all-to-all-start.1 = ((f32[4,1,40960]{2,1,0:T(1,128)}), f32[4,1,40960]{2,1,0:T(1,128)S(1)}, u32[]{:S(2)}, u32[]{:S(2)}) async-start(f32[4,1,40960]{2,1,0:T(1,128)} %reshape.301), calls=%async_computation.1 | async-start | bytes 1310720 | tf_op jit(solution)/shard_map/all_to_all | solution.py:144
Sparse Core Ops, SparseCore 0:
  702.5 68.6 all-reduce.2
where the time goes:
time: 877 us; the launch traced here: 876 us
  local copies, waits for them, and re-layouts  659 us (75%)
  waiting for transfers between devices  98.5 us (11%)
  other arithmetic  42 us (5%)
  blocking collectives  30.6 us (3%)
  starting transfers between devices  24.7 us (3%)
  between operations  15.1 us (2%)
    gather x8, local copies, waits for them, and re-layouts, on_device(): summed = summed + corner[None, :] * jnp.take(flattened, source, axis=1)  617 us
    unnamed x2, waiting for transfers between devices  68.8 us
    all_gather x1, blocking collectives, on_device(): lax.all_gather(change, 'lat', axis=0, tiled=True)  30.6 us
    unnamed x3, other arithmetic  21.6 us
    unnamed x37, local copies, waits for them, and re-layouts  18.4 us
  transfers between devices with their start and end apart: 13, of which 8 were waited for; matrix products, arithmetic and copies ran while one was open for 2% of the time, Pallas kernels for 0%

commit v1 on v0

--- a/solution.py
+++ b/solution.py
@@ -141,7 +141,10 @@
         precision=hp,
         preferred_element_type=jnp.float32,
     ).reshape(lev_local, rows_here, NLON)
-    increment = lax.all_to_all(circles, "lev", split_axis=2, concat_axis=0, tiled=True)
+    increment = jnp.concatenate(
+        lax.all_to_all(jnp.stack(jnp.split(circles, lax.axis_size("lev"), axis=2)), "lev", 0, 0),
+        axis=0,
+    )
     updated = advected + increment
     return (updated, damped)
 

time: 877 us -> 845 us (0.964)
  other arithmetic: 42 us -> 20 us
  local copies, waits for them, and re-layouts: 659 us -> 650 us
    unnamed x3 -> x2, other arithmetic: 21.6 us -> 2.18 us
    unnamed x37 -> x31, local copies, waits for them, and re-layouts: 18.4 us -> 6.64 us
  transfers between devices with their start and end apart: 13 -> 13, of which waited for: 8 -> 8; matrix products, arithmetic and copies ran while one was open for 2% -> 3% of each run, Pallas kernels for 0% -> 0%
where the time goes in v1:
time: 845 us; the launch traced here: 843 us
  local copies, waits for them, and re-layouts  650 us (77%)
  waiting for transfers between devices  99 us (12%)
  blocking collectives  30.6 us (4%)
  starting transfers between devices  25.2 us (3%)
  other arithmetic  20 us (2%)
  between operations  15 us (2%)
    gather x8, local copies, waits for them, and re-layouts, on_device(): summed = summed + corner[None, :] * jnp.take(flattened, source, axis=1)  619 us
    unnamed x2, waiting for transfers between devices  68.9 us
    all_gather x1, blocking collectives, on_device(): lax.all_gather(change, 'lat', axis=0, tiled=True)  30.6 us
  transfers between devices with their start and end apart: 13, of which 8 were waited for; matrix products, arithmetic and copies ran while one was open for 3% of the time, Pallas kernels for 0%

profile of v1, /device:TPU:0, one launch (start us, length us, event | category | flops | bytes accessed | tf_op | source)
XLA Modules:
  0.0 843.5 jit_solution(8111631968260475637)
XLA Ops:
  7.2 1.1 fusion.51
  8.3 4.9 collective-permute-start
  13.2 1.3 collective-permute-start.1
  14.5 1.1 fusion.42
  15.6 0.7 fusion.26
  16.6 0.7 fusion.24
  17.3 0.7 fusion.25
  18.0 0.7 compare_and_fusion.2
  18.8 1.1 convert_bitcast_fusion.3
  19.8 1.9 fusion.28
  21.8 1.3 select_reduce_fusion.1
  23.6 1.2 pad_maximum_fusion
  24.8 0.7 fusion.50
  25.5 1.7 collective-permute-start.3
  27.3 0.7 copy.74
  28.0 0.7 copy.76
  28.7 0.7 copy.78
  29.4 0.7 copy.80
  30.1 3.0 gather_fusion.5
  33.1 0.6 copy-done.7
  33.7 1.4 concatenate.13
  35.1 0.8 reshape.199
  35.9 11.2 %copy.56 = f32[4,45232]{0,1:T(8,128)} copy(f32[4,45232]{1,0:T(4,128)S(1)} %reshape.199) | data formatting | bytes 1447424 | tf_op jit(solution)/shard_map/reshape | solution.py:75
  47.2 142.8 %gather_fusion = f32[40960,4]{1,0:T(8,128)} fusion(f32[4,45232]{0,1:T(8,128)} %copy.56, s32[40960]{0:T(1024)S(1)} %copy-done.3), kind=kCustom, calls=%fused_computation.clone | custom fusion | bytes 1474560 | tf_op jit(solution)/shard_map/jit(_take)/gather | solution.py:83
  189.9 11.4 %copy.57 = f32[40960,4]{0,1:T(4,128)S(1)} copy(f32[40960,4]{1,0:T(8,128)} %gather_fusion) | data formatting | bytes 1310720 | tf_op jit(solution)/shard_map/jit(_take)/gather | solution.py:83
  201.4 142.8 %gather_fusion.1 = f32[40960,4]{1,0:T(8,128)} fusion(f32[4,45232]{0,1:T(8,128)} %copy.56, s32[40960]{0:T(1024)S(1)} %copy-done.4), kind=kCustom, calls=%fused_computation.3.clone | custom fusion | bytes 1474560 | tf_op jit(solution)/shard_map/jit(_take)/gather | solution.py:83
  344.2 12.1 %copy.59 = f32[40960,4]{0,1:T(4,128)} copy(f32[40960,4]{1,0:T(8,128)} %gather_fusion.1) | data formatting | bytes 1310720 | tf_op jit(solution)/shard_map/jit(_take)/gather | solution.py:83
  356.3 142.8 %gather_fusion.2 = f32[40960,4]{1,0:T(8,128)} fusion(f32[4,45232]{0,1:T(8,128)} %copy.56, s32[40960]{0:T(1024)S(1)} %copy-done.2), kind=kCustom, calls=%fused_computation.4.clone | custom fusion | bytes 1474560 | tf_op jit(solution)/shard_map/jit(_take)/gather | solution.py:83
  499.0 12.2 %copy.61 = f32[40960,4]{0,1:T(4,128)} copy(f32[40960,4]{1,0:T(8,128)} %gather_fusion.2) | data formatting | bytes 1310720 | tf_op jit(solution)/shard_map/jit(_take)/gather | solution.py:83
  511.2 142.8 %gather_fusion.3 = f32[40960,4]{1,0:T(8,128)} fusion(f32[4,45232]{0,1:T(8,128)} %copy.56, s32[40960]{0:T(1024)S(1)} %fusion.27), kind=kCustom, calls=%fused_computation.5.clone | custom fusion | bytes 1474560 | tf_op jit(solution)/shard_map/jit(_take)/gather | solution.py:83
  654.1 12.1 %copy.63 = f32[40960,4]{0,1:T(4,128)} copy(f32[40960,4]{1,0:T(8,128)} %gather_fusion.3) | data formatting | bytes 1310720 | tf_op jit(solution)/shard_map/jit(_take)/gather | solution.py:83
  666.2 2.6 fusion.1
  668.8 1.2 copy.96
  670.0 4.2 all-to-all-start
  674.6 1.1 maximum_multiply_fusion
  675.7 8.8 %all-to-all-done = f32[4,40,1024]{2,1,0:T(8,128)} async-done(((f32[4,40,1024]{2,1,0:T(8,128)}), f32[4,40,1024]{2,1,0:T(8,128)}, u32[]{:S(2)}, u32[]{:S(2)}) %all-to-all-start) | async-done | bytes 655392 | tf_op jit(solution)/shard_map/all_to_all | solution.py:91
  684.5 2.3 copy.64
  686.8 1.5 reshape.300
  688.3 0.6 convolution_convert_fusion
  689.0 2.7 collective-permute-start.4
  691.7 0.7 dynamic_slice.7
  692.4 1.0 collective-permute-done.4
  693.3 3.0 collective-permute-start.5
  696.4 1.6 collective-permute-done.5
  697.9 3.0 collective-permute-start.6
  701.0 1.2 dynamic-slice
  702.9 0.7 gather_fusion.4
  703.7 0.7 gather_fusion.6
  704.5 1.0 fusion.5
  705.4 1.0 select_bitcast_fusion.2
  706.4 0.7 pad_maximum_fusion.2
  707.2 68.8 %all-reduce.3.cloned.1.call-done = f32[16,2,1,2,640]{4,3,0,2,1:T(2,128)} async-done(((f32[16,2,1,2,640]{4,3,0,2,1:T(2,128)}), f32[16,2,1,2,640]{4,3,0,2,1:T(2,128)}) %all-reduce.3.cloned.1.call-update) | async-done | bytes 163856
  776.0 0.8 subtract_convert_fusion
  776.8 30.6 %all_gather.3 = bf16[16,2,1,2,640]{4,3,0,2,1:T(2,128)(2,1)S(1)} all-gather(bf16[2,2,1,2,640]{4,3,0,2,1:T(2,128)(2,1)S(1)} %get-tuple-element.17), channel_id=1, replica_groups=mesh['lat'=8,'lev'=4] {'lat'}, dimensions={0}, use_global_device_ids=true | all-gather | bytes 92160 | tf_op jit(solution)/shard_map/all_gather | solution.py:127
  808.2 3.3 collective-permute-done.7
  812.1 3.1 collective-permute-done.8
  815.4 1.7 cosine_multiply_fusion
  817.2 2.7 collective-permute-done.9
  820.0 0.7 convolution_bitcast_fusion
  820.8 0.9 pad_maximum_fusion.1
  821.7 3.5 all-to-all-start.1
  825.2 0.6 copy.71
  825.8 9.6 %all-to-all-done.1 = f32[4,1,40,1024]{3,2,1,0:T(8,128)S(1)} async-done(((f32[4,1,40,1024]{3,2,1,0:T(8,128)}), f32[4,1,40,1024]{3,2,1,0:T(8,128)S(1)}, u32[]{:S(2)}, u32[]{:S(2)}) %all-to-all-start.1) | async-done | bytes 655392 | tf_op jit(solution)/shard_map/all_to_all | solution.py:145
  835.4 1.2 bitcast_add_fusion
  (56 shorter events, 3.3 us)
Async XLA Ops:
  7.2 22.9 %copy-start = (bf16[40,16,640]{2,1,0:T(8,128)(2,1)S(1)}, bf16[40,16,640]{2,1,0:T(8,128)(2,1)}, u32[]{:S(2)}) copy-start(bf16[40,16,640]{2,1,0:T(8,128)(2,1)} %param.16) | copy-start | bytes 2457604
  8.3 15.4 %collective-permute-start = (f32[4,2,1024]{2,1,0:T(2,128)S(1)}, f32[4,2,1024]{2,1,0:T(2,128)S(1)}, u32[]{:S(2)}, u32[]{:S(2)}) collective-permute-start(f32[4,2,1024]{2,1,0:T(2,128)S(1)} %get-tuple-element.25), channel_id=1, source_target_pairs={{0,4},{4,8},{8,12},{12,16},{16,20},{20,24},{24,28},{1,5},{5,9},{9,... | collective-permute-start | bytes 98312 | tf_op jit(solution)/shard_map/ppermute | solution.py:20
  13.2 10.5 %collective-permute-start.1 = (f32[4,2,1024]{2,1,0:T(2,128)S(1)}, f32[4,2,1024]{2,1,0:T(2,128)S(1)}, u32[]{:S(2)}, u32[]{:S(2)}) collective-permute-start(f32[4,2,1024]{2,1,0:T(2,128)S(1)} %get-tuple-element.26), channel_id=1, source_target_pairs={{4,0},{8,4},{12,8},{16,12},{20,16},{24,20},{28,24},{5,1},{9,5},{13... | collective-permute-start | bytes 98312 | tf_op jit(solution)/shard_map/ppermute | solution.py:21
  25.5 7.5 collective-permute-start.2
  25.5 8.2 collective-permute-start.3
  27.3 5.8 copy-start.8
  33.0 14.1 %copy-start.3 = (s32[40960]{0:T(1024)S(1)}, s32[40960]{0:T(1024)}, u32[]{:S(2)}) copy-start(s32[40960]{0:T(1024)} %fusion.24) | copy-start | bytes 491524
  33.1 0.6 copy-start.7
  35.9 165.5 %copy-start.4 = (s32[40960]{0:T(1024)S(1)}, s32[40960]{0:T(1024)}, u32[]{:S(2)}) copy-start(s32[40960]{0:T(1024)} %fusion.25) | copy-start | bytes 491524
  189.9 166.3 %copy-start.2 = (s32[40960]{0:T(1024)S(1)}, s32[40960]{0:T(1024)}, u32[]{:S(2)}) copy-start(s32[40960]{0:T(1024)} %fusion.26) | copy-start | bytes 491524
  499.0 167.1 %copy-start.5 = (f32[5,8,8,128]{3,1,2,0:T(8,128)S(1)}, f32[5,8,8,128]{3,1,2,0:T(8,128)}, u32[]{:S(2)}) copy-start(f32[5,8,8,128]{3,1,2,0:T(8,128)} %copy.74) | copy-start | bytes 491524
  499.0 167.1 %copy-start.6 = (f32[5,8,8,128]{3,1,2,0:T(8,128)S(1)}, f32[5,8,8,128]{3,1,2,0:T(8,128)}, u32[]{:S(2)}) copy-start(f32[5,8,8,128]{3,1,2,0:T(8,128)} %copy.76) | copy-start | bytes 491524
  511.2 163.2 %copy-start.9 = (pred[16]{0:T(512)(128)(4,1)S(1)}, pred[16]{0:T(512)(128)(4,1)}, u32[]{:S(2)}) copy-start(pred[16]{0:T(512)(128)(4,1)} %compare_and_fusion.4) | copy-start | bytes 52
  511.2 325.4 %copy-start.1 = (bf16[40,16,640]{2,1,0:T(8,128)(2,1)S(1)}, bf16[40,16,640]{2,1,0:T(8,128)(2,1)}, u32[]{:S(2)}) copy-start(bf16[40,16,640]{2,1,0:T(8,128)(2,1)} %param.16) | copy-start | bytes 2457604
  670.0 14.5 %all-to-all-start = ((f32[4,40,1024]{2,1,0:T(8,128)}), f32[4,40,1024]{2,1,0:T(8,128)}, u32[]{:S(2)}, u32[]{:S(2)}) async-start(f32[4,40,1024]{2,1,0:T(8,128)} %bitcast.113), calls=%async_computation | async-start | bytes 1310720 | tf_op jit(solution)/shard_map/all_to_all | solution.py:91
  674.2 101.9 %all-reduce.3.cloned.1.call-start = ((), (), s32[]{:S(2)}) async-start(), calls=%async_computation.2 | async-start | bytes 327680
  689.0 4.3 collective-permute-start.4
  693.3 4.6 collective-permute-start.5
  697.9 5.7 collective-permute-start.6
  807.8 3.8 collective-permute-start.7
  811.5 3.7 collective-permute-start.8
  815.3 4.6 collective-permute-start.9
  821.7 13.7 %all-to-all-start.1 = ((f32[4,1,40,1024]{3,2,1,0:T(8,128)}), f32[4,1,40,1024]{3,2,1,0:T(8,128)S(1)}, u32[]{:S(2)}, u32[]{:S(2)}) async-start(f32[4,1,40,1024]{3,2,1,0:T(8,128)} %pad_maximum_fusion.1), calls=%async_computation.1 | async-start | bytes 1310720 | tf_op jit(solution)/shard_map/all_to_all | solution.py:145
Sparse Core Ops, SparseCore 0:
  707.3 68.6 all-reduce.2
